TPU v7x, 256 devices: a whole 4x4x8 slice. The times are simulated.
256 devices in a mesh: fsdp: 4 (over x), seq: 64 (over z, y, core).
Axes of the slice: x: 4, y: 4, z: 8, core: 2. Of those that a mesh axis runs over, the one named last changes fastest.
Arguments:
- tokens: bfloat16 [4, 16384, 4096], P('fsdp', 'seq'), may hold values from -6 to 6
- queries: bfloat16 [4, 16384, 4096], P('fsdp', 'seq'), may hold values from -70 to 70
- key_weight: bfloat16 [4096, 1024], P(('fsdp', 'seq')), may hold values from -0.09375 to 0.09375
- value_weight: bfloat16 [4096, 1024], P(('fsdp', 'seq')), may hold values from -0.09375 to 0.09375
- sorted_blocks: int32 [4, 8, 128], P('fsdp', None, 'seq'), may hold values from 0 to 127, as said below
Outputs:
- attended: bfloat16 [4, 16384, 4096], P('fsdp', 'seq')
Inputs may be any that keep to these rules, and one draw needn't show every extreme that they name: `sorted_blocks`: for each sequence and key-value head, a permutation of the 128 blocks. The 2 blocks of one device, over all key-value heads, name blocks that lie on one device at most 1 times, and for one head at most 1 times; both bounds are reached in every draw. Device d holds blocks d * 2 to d * 2 + 1.
All inputs are finite; a program needn't handle non-finite values.
Results may differ from a plain program's by a relative error of at most 0.012.
The roundings to bfloat16 on the way count: a program that leaves them out, or rounds other values in their place, can miss the bound.
Values may be sent and summed in bfloat16 or wider, within the bound.
A program may use at most 128 MiB of HBM per device.

v0:
```python
import math
import jax
import jax.numpy as jnp
from jax import lax
from jax.sharding import PartitionSpec as P

DH = 128
KVH = 8
GROUP = 4
BLOCK = 128


def shifted(value, axis, steps):
    count = lax.axis_size(axis)
    first, last = (max(0, -steps), min(count, count - steps))
    return lax.ppermute(value, axis, [(source, source + steps) for source in range(first, last)])


def fetch_blocks(kv_table, target_dev, target_row, devices, capacity, send_requests, send_blocks):
    item_count = target_dev.shape[0]
    item_order = jnp.arange(item_count, dtype=jnp.int32)
    same_dev = target_dev[:, None] == target_dev[None, :]
    earlier = item_order[None, :] < item_order[:, None]
    ranking = jnp.sum((same_dev & earlier).astype(jnp.int32), axis=1)
    dev_hit = target_dev[:, None, None] == jnp.arange(devices, dtype=jnp.int32)[None, :, None]
    slot_hit = ranking[:, None, None] == jnp.arange(capacity, dtype=jnp.int32)[None, None, :]
    requests = jnp.sum(jnp.where(dev_hit & slot_hit, (target_row + 1)[:, None, None], 0), axis=0)
    wanted = send_requests(requests)
    replies = jnp.take(kv_table, jnp.maximum(wanted - 1, 0), axis=0)
    replies = jnp.where((wanted > 0)[:, :, None, None], replies, jnp.zeros_like(replies))
    arrived = send_blocks(replies)
    arrived = arrived.reshape(devices * capacity, arrived.shape[2], arrived.shape[3])
    return jnp.take(arrived, target_dev * capacity + ranking, axis=0)


def local(tokens, queries, key_weight, value_weight, sorted_blocks):
    token_rows = tokens[0]
    local_tokens = token_rows.shape[0]
    local_blocks = local_tokens // BLOCK
    devices = lax.axis_size("seq")
    key_sums = jnp.dot(
        token_rows,
        lax.all_gather(key_weight, ("fsdp", "seq"), axis=0, tiled=True),
        preferred_element_type=jnp.float32,
    )
    value_sums = jnp.dot(
        token_rows,
        lax.all_gather(value_weight, ("fsdp", "seq"), axis=0, tiled=True),
        preferred_element_type=jnp.float32,
    )
    key_blocks = key_sums.astype(jnp.bfloat16).reshape(local_blocks, BLOCK, KVH, DH)
    value_blocks = value_sums.astype(jnp.bfloat16).reshape(local_blocks, BLOCK, KVH, DH)
    packed = jnp.concatenate([key_blocks, value_blocks], axis=3).transpose(2, 0, 1, 3)
    prev_edge = shifted(packed[:, local_blocks - 1], "seq", 1)
    preceding = jnp.concatenate([prev_edge[:, None], packed[:, : local_blocks - 1]], axis=1)
    targets = sorted_blocks[0]
    target_dev = targets // local_blocks
    target_slot = targets % local_blocks
    capacity = (local_blocks + devices - 1) // devices
    gathered_heads = []
    for kv_head in range(KVH):
        gathered_heads.append(
            fetch_blocks(
                packed[kv_head],
                target_dev[kv_head],
                target_slot[kv_head],
                devices,
                capacity,
                lambda payload: lax.all_to_all(
                    payload, "seq", split_axis=0, concat_axis=0, tiled=True
                ),
                lambda payload: lax.all_to_all(
                    payload, "seq", split_axis=0, concat_axis=0, tiled=True
                ),
            )
        )
    sorted_kv = jnp.stack(gathered_heads, axis=0)
    candidates = jnp.concatenate([packed, preceding, sorted_kv], axis=2)
    key_part = candidates[:, :, :, :DH]
    value_part = candidates[:, :, :, DH:]
    query_blocks = queries[0].reshape(local_blocks, BLOCK, KVH, GROUP, DH)
    scores = jnp.einsum(
        "bthge,hbke->hgbtk", query_blocks, key_part, preferred_element_type=jnp.float32
    ) * (1.0 / math.sqrt(DH))
    block_index = lax.axis_index("seq") * local_blocks + jnp.arange(local_blocks, dtype=jnp.int32)
    key_index = jnp.arange(3 * BLOCK, dtype=jnp.int32)
    blocked = (
        (block_index[:, None] == 0)
        & (key_index[None, :] >= BLOCK)
        & (key_index[None, :] < 2 * BLOCK)
    )
    scores = jnp.where(blocked[None, None, :, None, :], -1e30, scores)
    highest = jnp.max(scores, axis=-1, keepdims=True)
    raised = jnp.exp(scores - highest)
    weights = (raised / jnp.sum(raised, axis=-1, keepdims=True)).astype(jnp.bfloat16)
    result = jnp.einsum(
        "hgbtk,hbke->bthge", weights, value_part, preferred_element_type=jnp.float32
    )
    return result.astype(jnp.bfloat16).reshape(1, local_tokens, KVH * GROUP * DH)


def solution(mesh):
    placed = (
        P("fsdp", "seq", None),
        P("fsdp", "seq", None),
        P(("fsdp", "seq"), None),
        P(("fsdp", "seq"), None),
        P("fsdp", None, "seq"),
    )
    return jax.shard_map(
        local, mesh=mesh, in_specs=placed, out_specs=P("fsdp", "seq", None), check_vma=False
    )
```

profile of v0, /device:TPU:1, one launch (start us, length us, event | category | flops | bytes accessed | tf_op | source)
XLA Modules:
  0.0 1156.5 jit_solution(5378206535577151252)
XLA Ops:
  10.1 13.2 %all-to-all-start.14 = ((s32[64,1,1]{2,1,0:T(1,128)}), s32[64,1,1]{2,1,0:T(1,128)S(1)}, u32[]{:S(2)}, u32[]{:S(2)}) async-start(s32[64,1,1]{2,1,0:T(1,128)} %copy.82), calls=%async_computation.14 | async-start | bytes 65536 | tf_op jit(solution)/shard_map/all_to_all | solution.py:69
  33.3 10.3 all-to-all-start
  46.1 6.8 all-to-all-done
  57.6 9.5 all-to-all-done.2
  71.7 62.1 %all-gather.3.cloned.1.call-done = bf16[4096,1024]{1,0:T(8,128)(2,1)} async-done(((bf16[16,1024]{1,0:T(8,128)(2,1)}), bf16[4096,1024]{1,0:T(8,128)(2,1)}) %all-gather.3.cloned.1.call-update) | async-done | bytes 8388624 | tf_op jit(solution)/shard_map/all_gather | solution.py:43
  133.8 5.7 fusion.51
  139.5 6.9 all-to-all-start.6
  146.4 106.1 %all-gather.5.cloned.1.call-done = bf16[4096,1024]{1,0:T(8,128)(2,1)} async-done(((bf16[16,1024]{1,0:T(8,128)(2,1)}), bf16[4096,1024]{1,0:T(8,128)(2,1)}) %all-gather.5.cloned.1.call-update) | async-done | bytes 8388624 | tf_op jit(solution)/shard_map/all_gather | solution.py:48
  252.5 5.7 fusion.48
  258.7 6.9 all-to-all-start.8
  265.7 9.2 all-to-all-done.8
  275.0 4.7 all-to-all-start.10
  282.6 6.6 all-to-all-done.10
  297.8 5.5 all-to-all-done.12
  303.3 5.7 all-to-all-start.15
  318.3 85.4 %all-to-all-done.15 = bf16[64,1,128,256]{3,2,1,0:T(8,128)(2,1)} async-done(((bf16[64,1,128,256]{3,2,1,0:T(8,128)(2,1)}), bf16[64,1,128,256]{3,2,1,0:T(8,128)(2,1)}, u32[]{:S(2)}, u32[]{:S(2)}) %all-to-all-start.15) | async-done | bytes 4194336 | tf_op jit(solution)/shard_map/all_to_all | solution.py:72
  403.7 7.2 all-to-all-start.11
  420.1 85.4 %all-to-all-done.11 = bf16[64,1,128,256]{3,2,1,0:T(8,128)(2,1)} async-done(((bf16[64,1,128,256]{3,2,1,0:T(8,128)(2,1)}), bf16[64,1,128,256]{3,2,1,0:T(8,128)(2,1)}, u32[]{:S(2)}, u32[]{:S(2)}) %all-to-all-start.11) | async-done | bytes 4194336 | tf_op jit(solution)/shard_map/all_to_all | solution.py:72
  505.6 7.6 all-to-all-start.9
  522.4 85.2 %all-to-all-done.9 = bf16[64,1,128,256]{3,2,1,0:T(8,128)(2,1)} async-done(((bf16[64,1,128,256]{3,2,1,0:T(8,128)(2,1)}), bf16[64,1,128,256]{3,2,1,0:T(8,128)(2,1)}, u32[]{:S(2)}, u32[]{:S(2)}) %all-to-all-start.9) | async-done | bytes 4194336 | tf_op jit(solution)/shard_map/all_to_all | solution.py:72
  607.6 7.2 all-to-all-start.7
  624.0 85.5 %all-to-all-done.7 = bf16[64,1,128,256]{3,2,1,0:T(8,128)(2,1)} async-done(((bf16[64,1,128,256]{3,2,1,0:T(8,128)(2,1)}), bf16[64,1,128,256]{3,2,1,0:T(8,128)(2,1)}, u32[]{:S(2)}, u32[]{:S(2)}) %all-to-all-start.7) | async-done | bytes 4194336 | tf_op jit(solution)/shard_map/all_to_all | solution.py:72
  709.5 7.2 all-to-all-start.5
  726.0 85.5 %all-to-all-done.5 = bf16[64,1,128,256]{3,2,1,0:T(8,128)(2,1)} async-done(((bf16[64,1,128,256]{3,2,1,0:T(8,128)(2,1)}), bf16[64,1,128,256]{3,2,1,0:T(8,128)(2,1)}, u32[]{:S(2)}, u32[]{:S(2)}) %all-to-all-start.5) | async-done | bytes 4194336 | tf_op jit(solution)/shard_map/all_to_all | solution.py:72
  811.5 7.6 all-to-all-start.3
  828.3 85.3 %all-to-all-done.3 = bf16[64,1,128,256]{3,2,1,0:T(8,128)(2,1)} async-done(((bf16[64,1,128,256]{3,2,1,0:T(8,128)(2,1)}), bf16[64,1,128,256]{3,2,1,0:T(8,128)(2,1)}, u32[]{:S(2)}, u32[]{:S(2)}) %all-to-all-start.3) | async-done | bytes 4194336 | tf_op jit(solution)/shard_map/all_to_all | solution.py:72
  913.6 7.2 all-to-all-start.1
  930.2 85.3 %all-to-all-done.1 = bf16[64,1,128,256]{3,2,1,0:T(8,128)(2,1)} async-done(((bf16[64,1,128,256]{3,2,1,0:T(8,128)(2,1)}), bf16[64,1,128,256]{3,2,1,0:T(8,128)(2,1)}, u32[]{:S(2)}, u32[]{:S(2)}) %all-to-all-start.1) | async-done | bytes 4194336 | tf_op jit(solution)/shard_map/all_to_all | solution.py:72
  1015.5 7.2 all-to-all-start.13
  1058.8 59.7 %all-to-all-done.13 = bf16[64,1,128,256]{3,2,1,0:T(8,128)(2,1)} async-done(((bf16[64,1,128,256]{3,2,1,0:T(8,128)(2,1)}), bf16[64,1,128,256]{3,2,1,0:T(8,128)(2,1)}, u32[]{:S(2)}, u32[]{:S(2)}) %all-to-all-start.13) | async-done | bytes 4194336 | tf_op jit(solution)/shard_map/all_to_all | solution.py:72
  1123.3 9.2 fusion.80
  1132.5 7.9 convert_bitcast_fusion
  (144 shorter events, 151.7 us)
Async XLA Ops:
  6.5 127.2 %copy-start = (bf16[1,256,4096]{2,1,0:T(8,128)(2,1)S(1)}, bf16[1,256,4096]{2,1,0:T(8,128)(2,1)}, u32[]{:S(2)}) copy-start(bf16[1,256,4096]{2,1,0:T(8,128)(2,1)} %param.9) | copy-start | bytes 6291460
  6.5 127.2 %all-gather.3.cloned.1.call-start = ((), (), s32[]{:S(2)}) async-start(), calls=%async_computation.16 | async-start | bytes 8421376 | tf_op jit(solution)/shard_map/all_gather | solution.py:43
  7.3 245.3 %all-gather.5.cloned.1.call-start = ((), (), s32[]{:S(2)}) async-start(), calls=%async_computation.17 | async-start | bytes 8421376 | tf_op jit(solution)/shard_map/all_gather | solution.py:48
  10.1 23.2 %all-to-all-start.14 = ((s32[64,1,1]{2,1,0:T(1,128)}), s32[64,1,1]{2,1,0:T(1,128)S(1)}, u32[]{:S(2)}, u32[]{:S(2)}) async-start(s32[64,1,1]{2,1,0:T(1,128)} %copy.82), calls=%async_computation.14 | async-start | bytes 65536 | tf_op jit(solution)/shard_map/all_to_all | solution.py:69
  33.3 19.6 %all-to-all-start = ((s32[64,1,1]{2,1,0:T(1,128)}), s32[64,1,1]{2,1,0:T(1,128)S(1)}, u32[]{:S(2)}, u32[]{:S(2)}) async-start(s32[64,1,1]{2,1,0:T(1,128)} %copy.68), calls=%async_computation | async-start | bytes 65536 | tf_op jit(solution)/shard_map/all_to_all | solution.py:69
  52.9 14.1 %all-to-all-start.2 = ((s32[64,1,1]{2,1,0:T(1,128)}), s32[64,1,1]{2,1,0:T(1,128)S(1)}, u32[]{:S(2)}, u32[]{:S(2)}) async-start(s32[64,1,1]{2,1,0:T(1,128)} %copy.70), calls=%async_computation.2 | async-start | bytes 65536 | tf_op jit(solution)/shard_map/all_to_all | solution.py:69
  67.1 72.4 %all-to-all-start.4 = ((s32[64,1,1]{2,1,0:T(1,128)}), s32[64,1,1]{2,1,0:T(1,128)S(1)}, u32[]{:S(2)}, u32[]{:S(2)}) async-start(s32[64,1,1]{2,1,0:T(1,128)} %copy.72), calls=%async_computation.4 | async-start | bytes 65536 | tf_op jit(solution)/shard_map/all_to_all | solution.py:69
  139.5 119.2 %all-to-all-start.6 = ((s32[64,1,1]{2,1,0:T(1,128)}), s32[64,1,1]{2,1,0:T(1,128)S(1)}, u32[]{:S(2)}, u32[]{:S(2)}) async-start(s32[64,1,1]{2,1,0:T(1,128)} %copy.74), calls=%async_computation.6 | async-start | bytes 65536 | tf_op jit(solution)/shard_map/all_to_all | solution.py:69
  258.7 16.3 %all-to-all-start.8 = ((s32[64,1,1]{2,1,0:T(1,128)}), s32[64,1,1]{2,1,0:T(1,128)S(1)}, u32[]{:S(2)}, u32[]{:S(2)}) async-start(s32[64,1,1]{2,1,0:T(1,128)} %copy.76), calls=%async_computation.8 | async-start | bytes 65536 | tf_op jit(solution)/shard_map/all_to_all | solution.py:69
  275.0 14.2 %all-to-all-start.10 = ((s32[64,1,1]{2,1,0:T(1,128)}), s32[64,1,1]{2,1,0:T(1,128)S(1)}, u32[]{:S(2)}, u32[]{:S(2)}) async-start(s32[64,1,1]{2,1,0:T(1,128)} %copy.78), calls=%async_computation.10 | async-start | bytes 65536 | tf_op jit(solution)/shard_map/all_to_all | solution.py:69
  289.2 14.1 %all-to-all-start.12 = ((s32[64,1,1]{2,1,0:T(1,128)}), s32[64,1,1]{2,1,0:T(1,128)S(1)}, u32[]{:S(2)}, u32[]{:S(2)}) async-start(s32[64,1,1]{2,1,0:T(1,128)} %copy.80), calls=%async_computation.12 | async-start | bytes 65536 | tf_op jit(solution)/shard_map/all_to_all | solution.py:69
  303.3 100.3 %all-to-all-start.15 = ((bf16[64,1,128,256]{3,2,1,0:T(8,128)(2,1)}), bf16[64,1,128,256]{3,2,1,0:T(8,128)(2,1)}, u32[]{:S(2)}, u32[]{:S(2)}) async-start(bf16[64,1,128,256]{3,2,1,0:T(8,128)(2,1)} %fusion.13), calls=%async_computation.15 | async-start | bytes 8388608 | tf_op jit(solution)/shard_map/all_to_all | solution.py:72
  403.7 101.9 %all-to-all-start.11 = ((bf16[64,1,128,256]{3,2,1,0:T(8,128)(2,1)}), bf16[64,1,128,256]{3,2,1,0:T(8,128)(2,1)}, u32[]{:S(2)}, u32[]{:S(2)}) async-start(bf16[64,1,128,256]{3,2,1,0:T(8,128)(2,1)} %fusion.17), calls=%async_computation.11 | async-start | bytes 8388608 | tf_op jit(solution)/shard_map/all_to_all | solution.py:72
  505.6 102.1 %all-to-all-start.9 = ((bf16[64,1,128,256]{3,2,1,0:T(8,128)(2,1)}), bf16[64,1,128,256]{3,2,1,0:T(8,128)(2,1)}, u32[]{:S(2)}, u32[]{:S(2)}) async-start(bf16[64,1,128,256]{3,2,1,0:T(8,128)(2,1)} %fusion.19), calls=%async_computation.9 | async-start | bytes 8388608 | tf_op jit(solution)/shard_map/all_to_all | solution.py:72
  607.6 101.9 %all-to-all-start.7 = ((bf16[64,1,128,256]{3,2,1,0:T(8,128)(2,1)}), bf16[64,1,128,256]{3,2,1,0:T(8,128)(2,1)}, u32[]{:S(2)}, u32[]{:S(2)}) async-start(bf16[64,1,128,256]{3,2,1,0:T(8,128)(2,1)} %fusion.21), calls=%async_computation.7 | async-start | bytes 8388608 | tf_op jit(solution)/shard_map/all_to_all | solution.py:72
  709.5 101.9 %all-to-all-start.5 = ((bf16[64,1,128,256]{3,2,1,0:T(8,128)(2,1)}), bf16[64,1,128,256]{3,2,1,0:T(8,128)(2,1)}, u32[]{:S(2)}, u32[]{:S(2)}) async-start(bf16[64,1,128,256]{3,2,1,0:T(8,128)(2,1)} %fusion.23), calls=%async_computation.5 | async-start | bytes 8388608 | tf_op jit(solution)/shard_map/all_to_all | solution.py:72
  811.5 102.1 %all-to-all-start.3 = ((bf16[64,1,128,256]{3,2,1,0:T(8,128)(2,1)}), bf16[64,1,128,256]{3,2,1,0:T(8,128)(2,1)}, u32[]{:S(2)}, u32[]{:S(2)}) async-start(bf16[64,1,128,256]{3,2,1,0:T(8,128)(2,1)} %fusion.25), calls=%async_computation.3 | async-start | bytes 8388608 | tf_op jit(solution)/shard_map/all_to_all | solution.py:72
  913.6 101.9 %all-to-all-start.1 = ((bf16[64,1,128,256]{3,2,1,0:T(8,128)(2,1)}), bf16[64,1,128,256]{3,2,1,0:T(8,128)(2,1)}, u32[]{:S(2)}, u32[]{:S(2)}) async-start(bf16[64,1,128,256]{3,2,1,0:T(8,128)(2,1)} %fusion.27), calls=%async_computation.1 | async-start | bytes 8388608 | tf_op jit(solution)/shard_map/all_to_all | solution.py:72
  1015.5 103.1 %all-to-all-start.13 = ((bf16[64,1,128,256]{3,2,1,0:T(8,128)(2,1)}), bf16[64,1,128,256]{3,2,1,0:T(8,128)(2,1)}, u32[]{:S(2)}, u32[]{:S(2)}) async-start(bf16[64,1,128,256]{3,2,1,0:T(8,128)(2,1)} %fusion.15), calls=%async_computation.13 | async-start | bytes 8388608 | tf_op jit(solution)/shard_map/all_to_all | solution.py:72
  1028.8 92.6 %collective-permute-start = (bf16[8,128,256]{2,1,0:T(8,128)(2,1)}, bf16[8,128,256]{2,1,0:T(8,128)(2,1)S(1)}, u32[]{:S(2)}, u32[]{:S(2)}) collective-permute-start(bf16[8,128,256]{2,1,0:T(8,128)(2,1)} %get-tuple-element.39), channel_id=1, source_target_pairs={{0,1},{1,2},{2,3},{3,4},{4,5},{5,6},{6,7},{7,8},{8,9},{9,10},{10,1... | collective-permute-start | bytes 1572872 | tf_op jit(solution)/shard_map/ppermute | solution.py:16
  1132.5 16.9 %copy-start.1 = (bf16[1,256,4096]{2,1,0:T(8,128)(2,1)S(1)}, bf16[1,256,4096]{2,1,0:T(8,128)(2,1)}, u32[]{:S(2)}) copy-start(bf16[1,256,4096]{2,1,0:T(8,128)(2,1)} %param.9) | copy-start | bytes 6291460
Sparse Core Ops, SparseCore 0:
  11.1 122.6 all-gather.2
  137.5 115.0 all-gather.4
where the time goes:
time: 1170 us; the launch traced here: 1160 us
  waiting for transfers between devices  864 us (74%)
  starting transfers between devices  117 us (10%)
  local copies, waits for them, and re-layouts  66.5 us (6%)
  other arithmetic  66 us (6%)
  matrix products  28.5 us (2%)
  between operations  14.2 us (1%)
    all_to_all x16, waiting for transfers between devices, local(): lax.all_to_all(payload, 'seq', split_axis=0, concat_axis=0, tiled=True)  695 us
    all_to_all x16, starting transfers between devices, local(): lax.all_to_all(payload, 'seq', split_axis=0, concat_axis=0, tiled=True)  113 us
    all_gather x1, waiting for transfers between devices, local(): lax.all_gather(value_weight, ('fsdp', 'seq'), axis=0, tiled=True)  106 us
    all_gather x1, waiting for transfers between devices, local(): lax.all_gather(key_weight, ('fsdp', 'seq'), axis=0, tiled=True)  62.1 us
    select_n x8, other arithmetic, fetch_blocks(): jnp.where((wanted > 0)[:, :, None, None], replies, jnp.zeros_like(replies))  31.8 us
    gather x8, local copies, waits for them, and re-layouts, fetch_blocks(): return jnp.take(arrived, target_dev * capacity + ranking, axis=0)  23.9 us
  transfers between devices with their start and end apart: 19, of which 15 were waited for; matrix products, arithmetic and copies ran while one was open for 12% of the time, Pallas kernels for 0%

commit v1 on v0

--- a/solution.py
+++ b/solution.py
@@ -45,7 +45,15 @@
     )
     value_sums = jnp.dot(
         token_rows,
-        lax.all_gather(value_weight, ("fsdp", "seq"), axis=0, tiled=True),
+        jnp.concatenate(
+            jax.lax.all_to_all(
+                jnp.stack([value_weight] * jax.lax.axis_size(("fsdp", "seq")), 0),
+                ("fsdp", "seq"),
+                concat_axis=0,
+                split_axis=0,
+            ),
+            axis=0,
+        ),
         preferred_element_type=jnp.float32,
     )
     key_blocks = key_sums.astype(jnp.bfloat16).reshape(local_blocks, BLOCK, KVH, DH)

time: 1170 us -> 1220 us (1.043)
  waiting for transfers between devices: 864 us -> 897 us
  blocking collectives: 0 us -> 13.4 us
    all_to_all x0 -> x1, waiting for transfers between devices: none -> 195 us  [local(): jax.lax.all_to_all(jnp.stack([value_weight] * jax.lax.axis_size(('fsdp',...]
    all_gather x1 -> x0, waiting for transfers between devices: 106 us -> none  [local(): lax.all_gather(value_weight, ('fsdp', 'seq'), axis=0, tiled=True)]
    all_gather x1, waiting for transfers between devices: 62.1 us -> 0.02 us  [local(): lax.all_gather(key_weight, ('fsdp', 'seq'), axis=0, tiled=True)]
    all_to_all x0 -> x1, blocking collectives: none -> 13.4 us  [local(): lax.all_to_all(payload, 'seq', split_axis=0, concat_axis=0, tiled=True)]
    all_to_all x16 -> x15, starting transfers between devices: 113 us -> 104 us  [local(): lax.all_to_all(payload, 'seq', split_axis=0, concat_axis=0, tiled=True)]
    all_to_all x16 -> x15, waiting for transfers between devices: 695 us -> 702 us  [local(): lax.all_to_all(payload, 'seq', split_axis=0, concat_axis=0, tiled=True)]
  transfers between devices with their start and end apart: 19 -> 18, of which waited for: 15 -> 16; matrix products, arithmetic and copies ran while one was open for 12% -> 11% of each run, Pallas kernels for 0% -> 0%
where the time goes in v1:
time: 1220 us; the launch traced here: 1210 us
  waiting for transfers between devices  897 us (74%)
  starting transfers between devices  115 us (9%)
  local copies, waits for them, and re-layouts  71.1 us (6%)
  other arithmetic  67.6 us (6%)
  matrix products  28.5 us (2%)
  between operations  14.1 us (1%)
  blocking collectives  13.4 us (1%)
    all_to_all x15, waiting for transfers between devices, local(): lax.all_to_all(payload, 'seq', split_axis=0, concat_axis=0, tiled=True)  702 us
    all_to_all x1, waiting for transfers between devices, local(): jax.lax.all_to_all(jnp.stack([value_weight] * jax.lax.axis_size(('fsdp',...  195 us
    all_to_all x15, starting transfers between devices, local(): lax.all_to_all(payload, 'seq', split_axis=0, concat_axis=0, tiled=True)  104 us
    select_n x8, other arithmetic, fetch_blocks(): jnp.where((wanted > 0)[:, :, None, None], replies, jnp.zeros_like(replies))  31.9 us
  transfers between devices with their start and end apart: 18, of which 16 were waited for; matrix products, arithmetic and copies ran while one was open for 11% of the time, Pallas kernels for 0%

profile of v1, /device:TPU:1, one launch (start us, length us, event | category | flops | bytes accessed | tf_op | source)
XLA Modules:
  0.0 1207.3 jit_solution(10984194361841357628)
XLA Ops:
  8.8 13.2 %all-to-all-start.1 = ((s32[64,1,1]{2,1,0:T(1,128)}), s32[64,1,1]{2,1,0:T(1,128)S(1)}, u32[]{:S(2)}, u32[]{:S(2)}) async-start(s32[64,1,1]{2,1,0:T(1,128)} %copy.68), calls=%async_computation.1 | async-start | bytes 65536 | tf_op jit(solution)/shard_map/all_to_all | solution.py:77
  23.8 7.5 all-to-all-done.1
  36.1 9.3 all-to-all-done.3
  45.4 13.4 %all_to_all.117 = s32[64,1,1]{2,1,0:T(1,128)S(1)} all-to-all(s32[64,1,1]{2,1,0:T(1,128)S(1)} %copy.72), channel_id=1, replica_groups=mesh['fsdp'=4,'seq'=64] {'seq'}, dimensions={0} | all-to-all | bytes 512 | tf_op jit(solution)/shard_map/all_to_all | solution.py:77
  63.9 7.4 all-to-all-start
  82.1 194.5 %all-to-all-done = bf16[256,16,1024]{2,1,0:T(8,128)(2,1)} async-done(((bf16[256,16,1024]{2,1,0:T(8,128)(2,1)}), bf16[256,16,1024]{2,1,0:T(8,128)(2,1)}, u32[]{:S(2)}, u32[]{:S(2)}) %all-to-all-start) | async-done | bytes 8388640 | tf_op jit(solution)/shard_map/all_to_all | solution.py:49
  276.7 5.5 all-to-all-start.7
  282.2 5.7 fusion.48
  291.5 7.0 all-to-all-start.9
  298.6 5.7 fusion.51
  307.9 7.1 all-to-all-start.11
  315.2 9.2 all-to-all-done.11
  332.0 6.6 all-to-all-done.13
  347.3 5.5 all-to-all-done.15
  352.8 5.7 all-to-all-start.2
  367.7 85.4 %all-to-all-done.2 = bf16[64,1,128,256]{3,2,1,0:T(8,128)(2,1)} async-done(((bf16[64,1,128,256]{3,2,1,0:T(8,128)(2,1)}), bf16[64,1,128,256]{3,2,1,0:T(8,128)(2,1)}, u32[]{:S(2)}, u32[]{:S(2)}) %all-to-all-start.2) | async-done | bytes 4194336 | tf_op jit(solution)/shard_map/all_to_all | solution.py:80
  453.1 7.6 all-to-all-start.4
  470.0 85.2 %all-to-all-done.4 = bf16[64,1,128,256]{3,2,1,0:T(8,128)(2,1)} async-done(((bf16[64,1,128,256]{3,2,1,0:T(8,128)(2,1)}), bf16[64,1,128,256]{3,2,1,0:T(8,128)(2,1)}, u32[]{:S(2)}, u32[]{:S(2)}) %all-to-all-start.4) | async-done | bytes 4194336 | tf_op jit(solution)/shard_map/all_to_all | solution.py:80
  555.2 7.2 all-to-all-start.6
  571.6 85.5 %all-to-all-done.6 = bf16[64,1,128,256]{3,2,1,0:T(8,128)(2,1)} async-done(((bf16[64,1,128,256]{3,2,1,0:T(8,128)(2,1)}), bf16[64,1,128,256]{3,2,1,0:T(8,128)(2,1)}, u32[]{:S(2)}, u32[]{:S(2)}) %all-to-all-start.6) | async-done | bytes 4194336 | tf_op jit(solution)/shard_map/all_to_all | solution.py:80
  657.1 7.2 all-to-all-start.8
  673.6 85.4 %all-to-all-done.8 = bf16[64,1,128,256]{3,2,1,0:T(8,128)(2,1)} async-done(((bf16[64,1,128,256]{3,2,1,0:T(8,128)(2,1)}), bf16[64,1,128,256]{3,2,1,0:T(8,128)(2,1)}, u32[]{:S(2)}, u32[]{:S(2)}) %all-to-all-start.8) | async-done | bytes 4194336 | tf_op jit(solution)/shard_map/all_to_all | solution.py:80
  759.0 7.8 all-to-all-start.10
  776.1 85.2 %all-to-all-done.10 = bf16[64,1,128,256]{3,2,1,0:T(8,128)(2,1)} async-done(((bf16[64,1,128,256]{3,2,1,0:T(8,128)(2,1)}), bf16[64,1,128,256]{3,2,1,0:T(8,128)(2,1)}, u32[]{:S(2)}, u32[]{:S(2)}) %all-to-all-start.10) | async-done | bytes 4194336 | tf_op jit(solution)/shard_map/all_to_all | solution.py:80
  861.3 7.2 all-to-all-start.12
  878.0 85.2 %all-to-all-done.12 = bf16[64,1,128,256]{3,2,1,0:T(8,128)(2,1)} async-done(((bf16[64,1,128,256]{3,2,1,0:T(8,128)(2,1)}), bf16[64,1,128,256]{3,2,1,0:T(8,128)(2,1)}, u32[]{:S(2)}, u32[]{:S(2)}) %all-to-all-start.12) | async-done | bytes 4194336 | tf_op jit(solution)/shard_map/all_to_all | solution.py:80
  963.2 7.2 all-to-all-start.14
  979.7 85.4 %all-to-all-done.14 = bf16[64,1,128,256]{3,2,1,0:T(8,128)(2,1)} async-done(((bf16[64,1,128,256]{3,2,1,0:T(8,128)(2,1)}), bf16[64,1,128,256]{3,2,1,0:T(8,128)(2,1)}, u32[]{:S(2)}, u32[]{:S(2)}) %all-to-all-start.14) | async-done | bytes 4194336 | tf_op jit(solution)/shard_map/all_to_all | solution.py:80
  1065.1 7.2 all-to-all-start.16
  1108.5 59.7 %all-to-all-done.16 = bf16[64,1,128,256]{3,2,1,0:T(8,128)(2,1)} async-done(((bf16[64,1,128,256]{3,2,1,0:T(8,128)(2,1)}), bf16[64,1,128,256]{3,2,1,0:T(8,128)(2,1)}, u32[]{:S(2)}, u32[]{:S(2)}) %all-to-all-start.16) | async-done | bytes 4194336 | tf_op jit(solution)/shard_map/all_to_all | solution.py:80
  1174.1 9.2 fusion.80
  1183.3 7.9 convert_bitcast_fusion
  (145 shorter events, 164.0 us)
Async XLA Ops:
  6.5 275.7 %copy-start = (bf16[1,256,4096]{2,1,0:T(8,128)(2,1)S(1)}, bf16[1,256,4096]{2,1,0:T(8,128)(2,1)}, u32[]{:S(2)}) copy-start(bf16[1,256,4096]{2,1,0:T(8,128)(2,1)} %param.9) | copy-start | bytes 6291460
  8.8 22.5 %all-to-all-start.1 = ((s32[64,1,1]{2,1,0:T(1,128)}), s32[64,1,1]{2,1,0:T(1,128)S(1)}, u32[]{:S(2)}, u32[]{:S(2)}) async-start(s32[64,1,1]{2,1,0:T(1,128)} %copy.68), calls=%async_computation.1 | async-start | bytes 65536 | tf_op jit(solution)/shard_map/all_to_all | solution.py:77
  31.3 14.1 %all-to-all-start.3 = ((s32[64,1,1]{2,1,0:T(1,128)}), s32[64,1,1]{2,1,0:T(1,128)S(1)}, u32[]{:S(2)}, u32[]{:S(2)}) async-start(s32[64,1,1]{2,1,0:T(1,128)} %copy.70), calls=%async_computation.3 | async-start | bytes 65536 | tf_op jit(solution)/shard_map/all_to_all | solution.py:77
  63.9 212.8 %all-to-all-start = ((bf16[256,16,1024]{2,1,0:T(8,128)(2,1)}), bf16[256,16,1024]{2,1,0:T(8,128)(2,1)}, u32[]{:S(2)}, u32[]{:S(2)}) async-start(bf16[256,16,1024]{2,1,0:T(8,128)(2,1)} %stack.20), calls=%async_computation | async-start | bytes 16777216 | tf_op jit(solution)/shard_map/all_to_all | solution.py:49
  71.3 227.3 %all-gather.2.cloned.1.call-start = ((), (), s32[]{:S(2)}) async-start(), calls=%async_computation.17 | async-start | bytes 8421376 | tf_op jit(solution)/shard_map/all_gather | solution.py:43
  276.7 14.9 %all-to-all-start.7 = ((s32[64,1,1]{2,1,0:T(1,128)}), s32[64,1,1]{2,1,0:T(1,128)S(1)}, u32[]{:S(2)}, u32[]{:S(2)}) async-start(s32[64,1,1]{2,1,0:T(1,128)} %copy.74), calls=%async_computation.7 | async-start | bytes 65536 | tf_op jit(solution)/shard_map/all_to_all | solution.py:77
  291.5 16.4 %all-to-all-start.9 = ((s32[64,1,1]{2,1,0:T(1,128)}), s32[64,1,1]{2,1,0:T(1,128)S(1)}, u32[]{:S(2)}, u32[]{:S(2)}) async-start(s32[64,1,1]{2,1,0:T(1,128)} %copy.76), calls=%async_computation.9 | async-start | bytes 65536 | tf_op jit(solution)/shard_map/all_to_all | solution.py:77
  307.9 16.5 %all-to-all-start.11 = ((s32[64,1,1]{2,1,0:T(1,128)}), s32[64,1,1]{2,1,0:T(1,128)S(1)}, u32[]{:S(2)}, u32[]{:S(2)}) async-start(s32[64,1,1]{2,1,0:T(1,128)} %copy.78), calls=%async_computation.11 | async-start | bytes 65536 | tf_op jit(solution)/shard_map/all_to_all | solution.py:77
  324.4 14.2 %all-to-all-start.13 = ((s32[64,1,1]{2,1,0:T(1,128)}), s32[64,1,1]{2,1,0:T(1,128)S(1)}, u32[]{:S(2)}, u32[]{:S(2)}) async-start(s32[64,1,1]{2,1,0:T(1,128)} %copy.80), calls=%async_computation.13 | async-start | bytes 65536 | tf_op jit(solution)/shard_map/all_to_all | solution.py:77
  338.6 14.2 %all-to-all-start.15 = ((s32[64,1,1]{2,1,0:T(1,128)}), s32[64,1,1]{2,1,0:T(1,128)S(1)}, u32[]{:S(2)}, u32[]{:S(2)}) async-start(s32[64,1,1]{2,1,0:T(1,128)} %copy.82), calls=%async_computation.15 | async-start | bytes 65536 | tf_op jit(solution)/shard_map/all_to_all | solution.py:77
  352.8 100.4 %all-to-all-start.2 = ((bf16[64,1,128,256]{3,2,1,0:T(8,128)(2,1)}), bf16[64,1,128,256]{3,2,1,0:T(8,128)(2,1)}, u32[]{:S(2)}, u32[]{:S(2)}) async-start(bf16[64,1,128,256]{3,2,1,0:T(8,128)(2,1)} %fusion.27), calls=%async_computation.2 | async-start | bytes 8388608 | tf_op jit(solution)/shard_map/all_to_all | solution.py:80
  453.1 102.1 %all-to-all-start.4 = ((bf16[64,1,128,256]{3,2,1,0:T(8,128)(2,1)}), bf16[64,1,128,256]{3,2,1,0:T(8,128)(2,1)}, u32[]{:S(2)}, u32[]{:S(2)}) async-start(bf16[64,1,128,256]{3,2,1,0:T(8,128)(2,1)} %fusion.25), calls=%async_computation.4 | async-start | bytes 8388608 | tf_op jit(solution)/shard_map/all_to_all | solution.py:80
  555.2 101.9 %all-to-all-start.6 = ((bf16[64,1,128,256]{3,2,1,0:T(8,128)(2,1)}), bf16[64,1,128,256]{3,2,1,0:T(8,128)(2,1)}, u32[]{:S(2)}, u32[]{:S(2)}) async-start(bf16[64,1,128,256]{3,2,1,0:T(8,128)(2,1)} %fusion.23), calls=%async_computation.6 | async-start | bytes 8388608 | tf_op jit(solution)/shard_map/all_to_all | solution.py:80
  657.1 101.9 %all-to-all-start.8 = ((bf16[64,1,128,256]{3,2,1,0:T(8,128)(2,1)}), bf16[64,1,128,256]{3,2,1,0:T(8,128)(2,1)}, u32[]{:S(2)}, u32[]{:S(2)}) async-start(bf16[64,1,128,256]{3,2,1,0:T(8,128)(2,1)} %fusion.21), calls=%async_computation.8 | async-start | bytes 8388608 | tf_op jit(solution)/shard_map/all_to_all | solution.py:80
  759.0 102.3 %all-to-all-start.10 = ((bf16[64,1,128,256]{3,2,1,0:T(8,128)(2,1)}), bf16[64,1,128,256]{3,2,1,0:T(8,128)(2,1)}, u32[]{:S(2)}, u32[]{:S(2)}) async-start(bf16[64,1,128,256]{3,2,1,0:T(8,128)(2,1)} %fusion.19), calls=%async_computation.10 | async-start | bytes 8388608 | tf_op jit(solution)/shard_map/all_to_all | solution.py:80
  861.3 101.9 %all-to-all-start.12 = ((bf16[64,1,128,256]{3,2,1,0:T(8,128)(2,1)}), bf16[64,1,128,256]{3,2,1,0:T(8,128)(2,1)}, u32[]{:S(2)}, u32[]{:S(2)}) async-start(bf16[64,1,128,256]{3,2,1,0:T(8,128)(2,1)} %fusion.17), calls=%async_computation.12 | async-start | bytes 8388608 | tf_op jit(solution)/shard_map/all_to_all | solution.py:80
  963.2 101.9 %all-to-all-start.14 = ((bf16[64,1,128,256]{3,2,1,0:T(8,128)(2,1)}), bf16[64,1,128,256]{3,2,1,0:T(8,128)(2,1)}, u32[]{:S(2)}, u32[]{:S(2)}) async-start(bf16[64,1,128,256]{3,2,1,0:T(8,128)(2,1)} %fusion.15), calls=%async_computation.14 | async-start | bytes 8388608 | tf_op jit(solution)/shard_map/all_to_all | solution.py:80
  1065.1 103.1 %all-to-all-start.16 = ((bf16[64,1,128,256]{3,2,1,0:T(8,128)(2,1)}), bf16[64,1,128,256]{3,2,1,0:T(8,128)(2,1)}, u32[]{:S(2)}, u32[]{:S(2)}) async-start(bf16[64,1,128,256]{3,2,1,0:T(8,128)(2,1)} %fusion.13), calls=%async_computation.16 | async-start | bytes 8388608 | tf_op jit(solution)/shard_map/all_to_all | solution.py:80
  1078.5 93.9 %collective-permute-start = (bf16[8,128,256]{2,1,0:T(8,128)(2,1)}, bf16[8,128,256]{2,1,0:T(8,128)(2,1)S(1)}, u32[]{:S(2)}, u32[]{:S(2)}) collective-permute-start(bf16[8,128,256]{2,1,0:T(8,128)(2,1)} %get-tuple-element.39), channel_id=1, source_target_pairs={{0,1},{1,2},{2,3},{3,4},{4,5},{5,6},{6,7},{7,8},{8,9},{9,10},{10,1... | collective-permute-start | bytes 1572872 | tf_op jit(solution)/shard_map/ppermute | solution.py:16
  1102.6 71.6 %copy-start.2 = (pred[2,384]{1,0:T(4,128)(4,1)S(1)}, pred[2,384]{1,0:T(4,128)(4,1)}, u32[]{:S(2)}) copy-start(pred[2,384]{1,0:T(4,128)(4,1)} %and_and_fusion) | copy-start | bytes 2308
  1183.3 16.9 %copy-start.1 = (bf16[1,256,4096]{2,1,0:T(8,128)(2,1)S(1)}, bf16[1,256,4096]{2,1,0:T(8,128)(2,1)}, u32[]{:S(2)}) copy-start(bf16[1,256,4096]{2,1,0:T(8,128)(2,1)} %param.9) | copy-start | bytes 6291460
Sparse Core Ops, SparseCore 0:
  75.8 165.3 all-gather.1
